TPU v7x, 32 devices: a whole 2x2x4 slice. The times are simulated.
32 devices in a mesh: parts: 2 (over y), section: 2 (over core), tp: 8 (over z, x).
Axes of the slice: x: 2, y: 2, z: 4, core: 2. Of those that a mesh axis runs over, the one named last changes fastest.
Arguments:
- prompt_rows: bfloat16 [128, 8192], P(('parts', 'section', 'tp')), parts along dimension 0, may hold values from -72 to 72
- query_weight: bfloat16 [8192, 8192], P(None, 'tp'), may hold values from -0.0625 to 0.0625
- cache_weight: bfloat16 [8, 8192, 256], P('tp'), may hold values from -1 to 1, as said below
- output_weight: bfloat16 [8192, 8192], P('tp'), may hold values from -0.0625 to 0.0625
- documents: int32 [128], P('parts'), parts along dimension 0, may hold values from 0 to 3, never falling along the last dimension, each value on 1 to 32 neighbouring positions
- page_table: int32 [24], P('parts'), parts along dimension 0, may hold values from 0 to 15, as said below
Outputs:
- branch_output: bfloat16 [128, 8192], P(('parts', 'section', 'tp')), parts along dimension 0
- page_pool: bfloat16 [32, 8, 2048], P(('parts', 'section', 'tp')), parts along dimension 0
There are 2 independent parts, one for each index of `parts`. A program takes and returns all parts, laid end to end along the dimension named above; an argument that names none is the same for every part. Nothing has to cross between parts.
Inputs may be any that keep to these rules, and one draw needn't show every extreme that they name: `cache_weight`: entry t equals entry u whenever t == u. `documents`: ids never fall along the tokens; there are 4 prompts of 1 to 32 tokens, one of exactly 32. `page_table`: entries are distinct pool slots; slot q is owned by the device of index q along section+tp (one slot per device). Entries beyond the number of pages are not used.
All inputs are finite; a program needn't handle non-finite values.
Results may differ from a plain program's by a relative error of at most 0.0085.
The roundings to bfloat16 on the way count: a program that leaves them out, or rounds other values in their place, can miss the bound.
Values may be sent and summed in bfloat16 or wider, within the bound.
A program may use at most 64 MiB of HBM per device.

v0:
```python
import jax
import jax.numpy as jnp
from jax import lax
from jax.sharding import PartitionSpec as P

KV_HEADS = 8
HEAD = 128
PAGE = 8


rope_base = 500000.0


def from_partner(value, axis, distance):
    mask = 2**distance
    pairs = [(source, source ^ mask) for source in range(lax.axis_size(axis))]
    return lax.ppermute(value, axis, pairs)


def document_layout(documents):
    count = documents.shape[0]
    places = jnp.arange(count, dtype=jnp.int32)
    begins = jnp.concatenate([jnp.ones((1,), dtype=bool), documents[1:] != documents[:-1]])
    firsts = lax.cummax(jnp.where(begins, places, jnp.zeros_like(places)), axis=0)
    offsets = places - firsts
    starts = (offsets % PAGE == 0).astype(jnp.int32)
    pages = jnp.cumsum(starts) - 1
    return (offsets, pages)


def rope_tables(offsets, width):
    half_width = width // 2
    freqs = rope_base ** (-(jnp.arange(half_width, dtype=jnp.float32) * 2.0 / width))
    angles = offsets.astype(jnp.float32)[:, None] * freqs[None, :]
    return (jnp.cos(angles), jnp.sin(angles))


def rotate(values, cosines, sines):
    half_width = values.shape[-1] // 2
    first = values[..., :half_width]
    second = values[..., half_width:]
    return jnp.concatenate(
        [first * cosines - second * sines, second * cosines + first * sines], axis=-1
    )


def finish_cache(keyvals, cosines, sines):
    rotated = rotate(keyvals[:, :HEAD], cosines, sines)
    return jnp.concatenate([rotated, keyvals[:, HEAD:]], axis=1).astype(jnp.bfloat16)


def body(prompt_rows, query_weight, cache_weight, output_weight, documents, page_table):
    tp_count = lax.axis_size("tp")
    owners = lax.axis_size(("section", "tp"))
    section = lax.axis_index("section")
    column = lax.axis_index("tp")
    rows_dev = prompt_rows.shape[0]
    half_rows = rows_dev * tp_count
    total_rows = 2 * half_rows
    query_width = query_weight.shape[1]
    query_heads = query_width // HEAD
    replicas = tp_count // KV_HEADS
    slice_width = HEAD // replicas
    head_weight = cache_weight[0]
    offsets, pages = document_layout(documents)
    cosines, sines = rope_tables(offsets, HEAD)
    own_start = section * half_rows
    own_cos = lax.dynamic_slice_in_dim(cosines, own_start, half_rows, 0)
    own_sin = lax.dynamic_slice_in_dim(sines, own_start, half_rows, 0)
    piece = lax.all_gather(prompt_rows, "tp", axis=0, tiled=True)
    query_rows = jnp.dot(piece, query_weight, preferred_element_type=jnp.float32)
    cache_rows = jnp.dot(piece, head_weight, preferred_element_type=jnp.float32)
    joined = jnp.concatenate([query_rows, cache_rows], axis=1)
    query_part = joined[:, :query_width]
    cache_half = finish_cache(joined[:, query_width:], own_cos, own_sin)
    other = from_partner(cache_half, "section", 0)
    lower = jnp.where(section == 0, cache_half, other)
    upper = jnp.where(section == 0, other, cache_half)
    cache_all = jnp.concatenate([lower, upper], axis=0)
    queries = query_part.reshape(half_rows, query_heads, HEAD)
    queries = rotate(queries, own_cos[:, None, :], own_sin[:, None, :]).astype(jnp.bfloat16)
    keys = cache_all[:, :HEAD]
    values = cache_all[:, HEAD:]
    places = jnp.arange(total_rows, dtype=jnp.int32)
    query_places = own_start + jnp.arange(half_rows, dtype=jnp.int32)
    query_docs = lax.dynamic_slice_in_dim(documents, own_start, half_rows, 0)
    allowed = (query_docs[:, None] == documents[None, :]) & (
        places[None, :] <= query_places[:, None]
    )
    scale = 1.0 / HEAD**0.5
    scores = jnp.einsum("qhd,kd->hqk", queries, keys, preferred_element_type=jnp.float32) * scale
    scores = jnp.where(allowed[None, :, :], scores, -jnp.inf)
    weights = jax.nn.softmax(scores, axis=-1).astype(jnp.bfloat16)
    mixed = jnp.einsum("hqk,kd->qhd", weights, values, preferred_element_type=jnp.float32)
    attention = mixed.astype(jnp.bfloat16).reshape(half_rows, query_heads * HEAD)
    summed = lax.psum_scatter(
        jnp.dot(attention, output_weight, preferred_element_type=jnp.float32),
        "tp",
        scatter_dimension=0,
        tiled=True,
    )
    branch_output = summed.astype(jnp.bfloat16)
    column_start = section * HEAD + column % replicas * slice_width
    share = lax.dynamic_slice_in_dim(cache_all, column_start, slice_width, 1)
    capacity = rows_dev // 4 * PAGE
    row_of = page_table[pages] * PAGE + offsets % PAGE
    outgoing = jnp.zeros((owners * capacity, slice_width), jnp.bfloat16).at[row_of].set(share)
    outgoing = outgoing.reshape(owners, capacity, slice_width)
    arrived = lax.all_to_all(outgoing, ("section", "tp"), split_axis=0, concat_axis=2, tiled=True)
    return (branch_output, arrived)


def solution(mesh):
    return jax.shard_map(
        body,
        mesh=mesh,
        in_specs=(
            P(("parts", "section", "tp"), None),
            P(None, "tp"),
            P("tp", None, None),
            P("tp", None),
            P("parts"),
            P("parts"),
        ),
        out_specs=(P(("parts", "section", "tp"), None), P(("parts", "section", "tp"), None, None)),
        check_vma=False,
    )
```

profile of v0, /device:TPU:0, one launch (start us, length us, event | category | flops | bytes accessed | tf_op | source)
XLA Modules:
  0.0 150.3 jit_solution(4755525236660970167)
XLA Ops:
  0.6 0.0 copy-start.1
  0.6 0.0 copy-start
  0.7 1.8 %fusion.44 = (s32[1]{0:T(128)}, s32[1]{0:T(128)}, s32[1]{0:T(128)}, s32[1]{0:T(128)}, s32[1]{0:T(128)}, /*index=5*/s32[1]{0:T(128)}, s32[1]{0:T(128)}, s32[1]{0:...) fusion(s32[12]{0:T(128)} %param.11), kind=kLoop, calls=%fused_computation.74 | loop fusion | bytes 96 | tf_op jit(solution)/shard_map/gather | solution.py:106
  2.5 0.8 compare_bitcast_fusion
  3.3 0.1 add_select_fusion.1
  3.3 0.1 copy.18
  3.4 0.1 reduce-window.6
  3.6 0.1 reduce-window.9
  3.7 0.2 compare_reduce_fusion.4
  3.9 4.4 %select_reduce_fusion = s32[64]{0:T(128)S(1)} fusion(s32[]{:T(128)} %bitcast.12, s32[]{:T(128)} %bitcast.13, s32[]{:T(128)} %bitcast.14, s32[]{:T(128)} %bitcast.15, s32[]{:T(128)} %bitcast.16, s32[]{:T(128)} %bitcast.18, s32[]{:T(128)} %bitcast.17, s32[64,1]{1,0:T(8,128)S(1)} %reduce-window.9), kind=kLoop, calls=%fused_computation.35 | loop fusion | flops 1024 | bytes 540 | tf_op jit(solution)/shard_map/gather | solution.py:106
  8.3 3.2 %fusion.31 = s32[64,1]{0,1:T(1,128)S(1)} fusion(pred[64]{0:T(512)(128)(4,1)S(1)} %get-tuple-element.8, pred[64]{0:T(512)(128)(4,1)S(1)} %get-tuple-element.5, pred[64]{0:T(512)(128)(4,1)S(1)} %get-tuple-element.6, pred[64]{0:T(512)(128)(4,1)S(1)} %get-tuple-element.7, pred[64]{0:T(512)(128)(4,1)S(1)} %get-tuple-element.4, s32[64]{0:T(128)S(1)} %select_reduce_fusion, ...), kind=kLoop, calls=%fused_computation.63 | loop fusion | flops 384 | bytes 852 | tf_op jit(solution)/shard_map/mul | solution.py:106
  11.5 0.1 copy.22
  11.6 0.1 fusion.15
  11.7 33.3 %all-gather = bf16[8,4,8192]{2,1,0:T(4,128)(2,1)S(1)} all-gather(bf16[1,4,8192]{2,1,0:T(4,128)(2,1)} %bitcast.64), channel_id=1, replica_groups=mesh['parts'=2,'section'=2,'tp'=8] {'tp'}, dimensions={0}, use_global_device_ids=true | all-gather | bytes 589824 | tf_op jit(solution)/shard_map/all_gather | solution.py:70
  45.0 0.1 reshape.264
  45.1 3.0 %fusion.1 = f32[32,256]{1,0:T(8,128)S(1)} fusion(bf16[32,8192]{1,0:T(8,128)(2,1)S(1)} %reshape.264, bf16[1,8192,256]{2,1,0:T(8,128)(2,1)} %param.8), kind=kOutput, calls=%fused_computation.2 | convolution fusion | flops 134217728 | bytes 4751360 | tf_op jit(solution)/shard_map/dot_general | solution.py:72
  48.2 0.1 broadcast_multiply_fusion
  48.2 0.1 subtract_convert_fusion.1
  48.3 0.1 add_convert_fusion.1
  48.4 0.1 pad_maximum_fusion
  48.5 0.0 collective-permute-start
  48.5 0.7 dynamic_slice.14
  49.2 8.7 %convolution_bitcast_fusion = f32[4,8,8,128]{3,1,2,0:T(8,128)S(1)} fusion(bf16[32,8192]{1,0:T(8,128)(2,1)S(1)} %reshape.264, bf16[8192,1024]{1,0:T(8,128)(2,1)} %param.7), kind=kOutput, calls=%fused_computation.6 | convolution fusion | flops 536870912 | bytes 17432576 | tf_op jit(solution)/shard_map/dot_general | solution.py:71
  58.0 0.1 fusion.43
  58.1 0.1 subtract_convert_fusion
  58.2 0.0 copy-done
  58.2 0.1 fusion.26
  58.3 0.0 copy-done.1
  58.3 0.6 dynamic-slice
  59.5 0.0 collective-permute-done
  59.5 0.1 broadcast_select_fusion
  59.6 1.3 scatter_custom_fusion
  60.9 5.8 %all-to-all-start = ((bf16[16,8,128]{2,1,0:T(8,128)(2,1)}), bf16[16,8,128]{2,1,0:T(8,128)(2,1)S(1)}, u32[]{:S(2)}, u32[]{:S(2)}) async-start(bf16[16,8,128]{2,1,0:T(8,128)(2,1)} %bitcast.20), calls=%async_computation | async-start | bytes 65536 | tf_op jit(solution)/shard_map/all_to_all | solution.py:109
  66.7 0.4 fusion.45
  67.2 0.2 fusion.7
  67.4 8.7 %fusion.8 = f32[32,8192]{1,0:T(8,128)S(1)} fusion(bf16[1024,8192]{1,0:T(8,128)(2,1)} %param.9, bf16[8,4,8,128]{3,2,1,0:T(8,128)(2,1)S(1)} %fusion.7), kind=kOutput, calls=%fused_computation.18 | convolution fusion | flops 536870912 | bytes 17891328 | tf_op jit(solution)/shard_map/dot_general | solution.py:97
  76.1 72.9 %all-reduce.2 = bf16[32,8192]{1,0:T(8,128)(2,1)S(1)} all-reduce(f32[32,8192]{1,0:T(8,128)S(1)} %fusion.8), channel_id=2, replica_groups=mesh['parts'=2,'section'=2,'tp'=8] {'tp'}, use_global_device_ids=true, to_apply=%region_3.4.clone | all-reduce | flops 262144 | bytes 1572864
  149.0 0.7 dynamic-slice_convert_fusion
  149.7 0.0 all-to-all-done
  149.7 0.6 copy.45
  (6 shorter events, 0.1 us)
Async XLA Ops:
  0.6 57.6 %copy-start.1 = (u32[32]{0:T(128)S(1)}, u32[32]{0:T(128)}, u32[]{:S(2)}) copy-start(u32[32]{0:T(128)} %constant.96) | copy-start | bytes 388
  0.6 57.5 %copy-start = (s32[64]{0:T(128)S(1)}, s32[64]{0:T(128)}, u32[]{:S(2)}) copy-start(s32[64]{0:T(128)} %param.10) | copy-start | bytes 772
  48.5 11.0 %collective-permute-start = (bf16[32,256]{1,0:T(8,128)(2,1)S(1)}, bf16[32,256]{1,0:T(8,128)(2,1)S(1)}, u32[]{:S(2)}, u32[]{:S(2)}) collective-permute-start(bf16[32,256]{1,0:T(8,128)(2,1)S(1)} %pad_maximum_fusion), channel_id=1, source_target_pairs={{0,8},{8,0},{1,9},{9,1},{2,10},{10,2},{3,11},{11,3},{4,12},{12,4},... | collective-permute-start | bytes 49160 | tf_op jit(solution)/shard_map/ppermute | solution.py:17
  60.9 88.8 %all-to-all-start = ((bf16[16,8,128]{2,1,0:T(8,128)(2,1)}), bf16[16,8,128]{2,1,0:T(8,128)(2,1)S(1)}, u32[]{:S(2)}, u32[]{:S(2)}) async-start(bf16[16,8,128]{2,1,0:T(8,128)(2,1)} %bitcast.20), calls=%async_computation | async-start | bytes 65536 | tf_op jit(solution)/shard_map/all_to_all | solution.py:109
where the time goes:
time: 151 us; the launch traced here: 150 us
  blocking collectives  106 us (70%)
  matrix products  21.1 us (14%)
  other arithmetic  10.9 us (7%)
  starting transfers between devices  5.83 us (4%)
  local copies, waits for them, and re-layouts  4.85 us (3%)
    unnamed x1, blocking collectives  72.9 us
    all_gather x1, blocking collectives, body(): piece = lax.all_gather(prompt_rows, 'tp', axis=0, tiled=True)  33.3 us
    dot_general x1, matrix products, body(): jnp.dot(attention, output_weight, preferred_element_type=jnp.float32)  8.75 us
    dot_general x1, matrix products, body(): jnp.dot(piece, query_weight, preferred_element_type=jnp.float32)  8.75 us
    all_to_all x1, starting transfers between devices, body(): lax.all_to_all(outgoing, ('section', 'tp'), split_axis=0, concat_axis=2,...  5.82 us
    gather x2, other arithmetic, body(): row_of = page_table[pages] * PAGE + offsets % PAGE  4.6 us
    mul x1, other arithmetic, body(): row_of = page_table[pages] * PAGE + offsets % PAGE  3.23 us
  transfers between devices with their start and end apart: 2, of which 0 were waited for; matrix products, arithmetic and copies ran while one was open for 14% of the time, Pallas kernels for 0%

commit v1 on v0

--- a/solution.py
+++ b/solution.py
@@ -1,11 +1,19 @@
+import functools
+import math
+
 import jax
 import jax.numpy as jnp
 from jax import lax
+from jax.experimental import pallas as pl
+from jax.experimental.pallas import tpu as pltpu
 from jax.sharding import PartitionSpec as P
 
 KV_HEADS = 8
 HEAD = 128
 PAGE = 8
+K_CHUNKS = 4
+N_CHUNKS = 4
+MESH = pl.DeviceIdType.MESH
 
 
 rope_base = 500000.0
@@ -110,9 +118,354 @@
     return (branch_output, arrived)
 
 
+def fused_kernel(
+    sizes,
+    rows_hbm,
+    wq_hbm,
+    wkv_hbm,
+    wo_hbm,
+    docs_ref,
+    table_ref,
+    out_ref,
+    pool_ref,
+    xbuf,
+    wq,
+    wkv,
+    wo,
+    acc_q,
+    acc_kv,
+    kv_all,
+    pagebuf,
+    pagerecv,
+    attn,
+    sendbuf,
+    recvbuf,
+    x_send,
+    x_recv,
+    x_local,
+    w_sem,
+    wo_sem,
+    kv_send,
+    kv_recv,
+    page_send,
+    page_recv,
+    page_local,
+    r_send,
+    r_recv,
+):
+    tp_count, section_count, k_chunks, n_chunks = sizes
+    part = lax.axis_index("parts")
+    section = lax.axis_index("section")
+    me = lax.axis_index("tp")
+    rows_dev, depth = rows_hbm.shape
+    half_rows = rows_dev * tp_count
+    total_rows = section_count * half_rows
+    kc = depth // k_chunks
+    width = wq_hbm.shape[1]
+    heads = width // HEAD
+    out_width = wo_hbm.shape[1]
+    nc = out_width // n_chunks
+    owners = section_count * tp_count
+
+    def peer(distance):
+        return lax.rem(me + distance, tp_count)
+
+    def device(sec, col):
+        return (part, sec, col)
+
+    barrier = pltpu.get_barrier_semaphore()
+    for sec in range(section_count):
+        for distance in range(tp_count):
+            if sec == 0 and distance == 0:
+                continue
+            target = device(lax.rem(section + sec, section_count), peer(distance))
+            pl.semaphore_signal(barrier, inc=1, device_id=target, device_id_type=MESH)
+
+    def weight_copies(c):
+        where = pl.ds(c * kc, kc)
+        return (
+            pltpu.make_async_copy(wkv_hbm.at[0, where], wkv.at[c], w_sem.at[c, 0]),
+            pltpu.make_async_copy(wq_hbm.at[where], wq.at[c], w_sem.at[c, 1]),
+        )
+
+    def out_copy(n):
+        return pltpu.make_async_copy(
+            wo_hbm.at[:, pl.ds(pl.multiple_of(n * nc, nc), nc)], wo.at[n], wo_sem.at[n]
+        )
+
+    def row_copy(c, distance):
+        return pltpu.make_async_remote_copy(
+            src_ref=rows_hbm.at[:, pl.ds(pl.multiple_of(c * kc, kc), kc)],
+            dst_ref=xbuf.at[c, me],
+            send_sem=x_send.at[c, distance],
+            recv_sem=x_recv.at[c, distance],
+            device_id=device(section, peer(distance)),
+            device_id_type=MESH,
+        )
+
+    def own_rows(c):
+        return pltpu.make_async_copy(
+            rows_hbm.at[:, pl.ds(pl.multiple_of(c * kc, kc), kc)], xbuf.at[c, me], x_local.at[c]
+        )
+
+    for copy in weight_copies(0):
+        copy.start()
+    for c in range(k_chunks):
+        own_rows(c).start()
+    pl.semaphore_wait(barrier, owners - 1)
+    for c in range(k_chunks):
+        for distance in range(1, tp_count):
+            row_copy(c, distance).start()
+    for c in range(1, k_chunks):
+        for copy in weight_copies(c):
+            copy.start()
+    for n in range(n_chunks):
+        out_copy(n).start()
+
+    docs = docs_ref[...].astype(jnp.float32)
+    table = table_ref[...].astype(jnp.float32)
+
+    def iota(shape, axis):
+        return lax.broadcasted_iota(jnp.int32, shape, axis)
+
+    def layout(count, start):
+        row_at = iota((count, total_rows), 0) + start
+        col_at = iota((count, total_rows), 1)
+        own = jnp.sum(jnp.where(row_at == col_at, docs, 0.0), axis=1, keepdims=True)
+        return row_at, col_at, own == docs
+
+    def mod_page(values):
+        return values - PAGE * jnp.floor(values * (1.0 / PAGE))
+
+    row_at, col_at, same = layout(half_rows, section * half_rows)
+    allowed = same & (col_at <= row_at)
+    offset_own = jnp.sum(jnp.where(same & (col_at < row_at), 1.0, 0.0), axis=1, keepdims=True)
+    lane = iota((half_rows, HEAD), 1)
+    half = HEAD // 2
+    second = lane >= half
+    freq_at = jnp.where(second, lane - half, lane).astype(jnp.float32)
+    freqs = jnp.exp(freq_at * (-2.0 / HEAD * math.log(rope_base)))
+    angles = offset_own * freqs
+    cosines = jnp.cos(angles)
+    sines = jnp.sin(angles)
+    sines = jnp.where(second, sines, -sines)
+
+    row_at, col_at, same = layout(total_rows, 0)
+    offset_col = jnp.sum(jnp.where(same & (col_at < row_at), 1.0, 0.0), axis=1, keepdims=True)
+    offset_row = jnp.sum(jnp.where(same & (row_at < col_at), 1.0, 0.0), axis=0, keepdims=True)
+    begins = jnp.where((mod_page(offset_col) == 0.0) & (row_at <= col_at), 1.0, 0.0)
+    page_row = jnp.sum(begins, axis=0, keepdims=True) - 1.0
+    slot_row = jnp.zeros_like(page_row)
+    for p in range(table_ref.shape[1]):
+        slot_row += jnp.where(page_row == float(p), table[:, p : p + 1], 0.0)
+    place_row = slot_row * PAGE + mod_page(offset_row)
+    place_at = iota((owners * PAGE, total_rows), 0).astype(jnp.float32)
+    select = jnp.where(place_at == place_row, 1.0, 0.0).astype(jnp.bfloat16)
+
+    def rotate_rows(values):
+        return values * cosines + pltpu.roll(values, half, 1) * sines
+
+    acc_q[...] = jnp.zeros_like(acc_q)
+    acc_kv[...] = jnp.zeros_like(acc_kv)
+
+    def project(c, carry):
+        own_rows(c).wait()
+        for distance in range(1, tp_count):
+            row_copy(c, distance).wait_recv()
+        pieces = [xbuf[c, t].astype(jnp.float32) for t in range(tp_count)]
+        block = jnp.concatenate(pieces, axis=0).astype(jnp.bfloat16)
+        copies = weight_copies(c)
+        copies[0].wait()
+        acc_kv[...] += jnp.dot(block, wkv[c], preferred_element_type=jnp.float32)
+        copies[1].wait()
+        acc_q[...] += jnp.dot(block, wq[c], preferred_element_type=jnp.float32)
+        return carry
+
+    lax.fori_loop(0, k_chunks, project, 0)
+
+    keys_own = rotate_rows(acc_kv[:, :HEAD])
+    kv_all[section] = jnp.concatenate([keys_own, acc_kv[:, HEAD:]], axis=1).astype(jnp.bfloat16)
+    kv_copy = pltpu.make_async_remote_copy(
+        src_ref=kv_all.at[section],
+        dst_ref=kv_all.at[section],
+        send_sem=kv_send,
+        recv_sem=kv_recv,
+        device_id=device(1 - section, me),
+        device_id_type=MESH,
+    )
+    kv_copy.start()
+    queries = jnp.concatenate(
+        [rotate_rows(acc_q[:, h * HEAD : (h + 1) * HEAD]) for h in range(heads)], axis=0
+    ).astype(jnp.bfloat16)
+    kv_copy.wait()
+    both = jnp.concatenate([kv_all[0], kv_all[1]], axis=0)
+
+    paged = jnp.dot(select, both, preferred_element_type=jnp.float32).astype(jnp.bfloat16)
+    for kind in range(2):
+        for q in range(owners):
+            pagebuf[kind, q] = paged[q * PAGE : (q + 1) * PAGE, kind * HEAD : (kind + 1) * HEAD]
+    own_slot = section * tp_count + me
+
+    def page_copy(sec, distance):
+        sec_to = lax.rem(section + sec, section_count)
+        to = peer(distance)
+        return pltpu.make_async_remote_copy(
+            src_ref=pagebuf.at[section, sec_to * tp_count + to],
+            dst_ref=pagerecv.at[own_slot],
+            send_sem=page_send.at[sec, distance],
+            recv_sem=page_recv.at[sec, distance],
+            device_id=device(sec_to, to),
+            device_id_type=MESH,
+        )
+
+    others = [
+        (sec, distance)
+        for sec in range(section_count)
+        for distance in range(tp_count)
+        if sec or distance
+    ]
+    for sec, distance in others:
+        page_copy(sec, distance).start()
+    own_page = pltpu.make_async_copy(
+        pagebuf.at[section, own_slot], pagerecv.at[own_slot], page_local
+    )
+    own_page.start()
+
+    keys = both[:, :HEAD]
+    values = both[:, HEAD:]
+    scores = lax.dot_general(
+        queries, keys, (((1,), (1,)), ((), ())), preferred_element_type=jnp.float32
+    ) * (1.0 / HEAD**0.5)
+    keep = jnp.concatenate([jnp.where(allowed, 1.0, 0.0)] * heads, axis=0)
+    scores = jnp.where(keep > 0.5, scores, -jnp.inf)
+    top = jnp.max(scores, axis=1, keepdims=True)
+    powers = jnp.exp(scores - top)
+    weights = (powers / jnp.sum(powers, axis=1, keepdims=True)).astype(jnp.bfloat16)
+    mixed = jnp.dot(weights, values, preferred_element_type=jnp.float32).astype(jnp.bfloat16)
+    for h in range(heads):
+        attn[:, h * HEAD : (h + 1) * HEAD] = mixed[h * half_rows : (h + 1) * half_rows]
+
+    def sum_copy(n, distance):
+        to = peer(distance)
+        return pltpu.make_async_remote_copy(
+            src_ref=sendbuf.at[n, to],
+            dst_ref=recvbuf.at[n, me],
+            send_sem=r_send.at[n, distance],
+            recv_sem=r_recv.at[n, distance],
+            device_id=device(section, to),
+            device_id_type=MESH,
+        )
+
+    def produce(n, carry):
+        out_copy(n).wait()
+        partial = jnp.dot(attn[...], wo[n], preferred_element_type=jnp.float32)
+        for t in range(tp_count):
+            sendbuf[n, t] = partial[t * rows_dev : (t + 1) * rows_dev].astype(jnp.bfloat16)
+        for distance in range(1, tp_count):
+            sum_copy(n, distance).start()
+        return carry
+
+    lax.fori_loop(0, n_chunks, produce, 0)
+
+    own_page.wait()
+    for sec, distance in others:
+        page_copy(sec, distance).wait()
+    for slot in range(owners):
+        pool_ref[0, :, slot * HEAD : (slot + 1) * HEAD] = pagerecv[slot]
+
+    for n in range(n_chunks):
+        total = sendbuf[n, me].astype(jnp.float32)
+        for distance in range(1, tp_count):
+            sum_copy(n, distance).wait_recv()
+            source = lax.rem(me + tp_count - distance, tp_count)
+            total += recvbuf[n, source].astype(jnp.float32)
+        out_ref[:, n * nc : (n + 1) * nc] = total.astype(jnp.bfloat16)
+
+    for c in range(k_chunks):
+        for distance in range(1, tp_count):
+            row_copy(c, distance).wait_send()
+    for n in range(n_chunks):
+        for distance in range(1, tp_count):
+            sum_copy(n, distance).wait_send()
+
+
+def fused_body(prompt_rows, query_weight, cache_weight, output_weight, documents, page_table):
+    tp_count = lax.axis_size("tp")
+    section_count = lax.axis_size("section")
+    rows_dev, depth = prompt_rows.shape
+    width = query_weight.shape[1]
+    out_width = output_weight.shape[1]
+    half_rows = rows_dev * tp_count
+    owners = section_count * tp_count
+    k_chunks = K_CHUNKS
+    n_chunks = N_CHUNKS
+    kc, nc = depth // k_chunks, out_width // n_chunks
+    bf16, f32 = jnp.bfloat16, jnp.float32
+    dma = pltpu.SemaphoreType.DMA
+    anywhere = pl.BlockSpec(memory_space=pl.ANY)
+    local = pl.BlockSpec(memory_space=pltpu.VMEM)
+    return pl.pallas_call(
+        functools.partial(fused_kernel, (tp_count, section_count, k_chunks, n_chunks)),
+        out_shape=(
+            jax.ShapeDtypeStruct((rows_dev, out_width), bf16),
+            jax.ShapeDtypeStruct((1, PAGE, owners * HEAD), bf16),
+        ),
+        in_specs=[anywhere] * 4 + [local] * 2,
+        out_specs=(local, local),
+        scratch_shapes=[
+            pltpu.VMEM((k_chunks, tp_count, rows_dev, kc), bf16),
+            pltpu.VMEM((k_chunks, kc, width), bf16),
+            pltpu.VMEM((k_chunks, kc, 2 * HEAD), bf16),
+            pltpu.VMEM((n_chunks, width, nc), bf16),
+            pltpu.VMEM((half_rows, width), f32),
+            pltpu.VMEM((half_rows, 2 * HEAD), f32),
+            pltpu.VMEM((section_count, half_rows, 2 * HEAD), bf16),
+            pltpu.VMEM((2, owners, PAGE, HEAD), bf16),
+            pltpu.VMEM((owners, PAGE, HEAD), bf16),
+            pltpu.VMEM((half_rows, width), bf16),
+            pltpu.VMEM((n_chunks, tp_count, rows_dev, nc), bf16),
+            pltpu.VMEM((n_chunks, tp_count, rows_dev, nc), bf16),
+            dma((k_chunks, tp_count)),
+            dma((k_chunks, tp_count)),
+            dma((k_chunks,)),
+            dma((k_chunks, 2)),
+            dma((n_chunks,)),
+            dma,
+            dma,
+            dma((section_count, tp_count)),
+            dma((section_count, tp_count)),
+            dma,
+            dma((n_chunks, tp_count)),
+            dma((n_chunks, tp_count)),
+        ],
+        compiler_params=pltpu.CompilerParams(
+            collective_id=0, has_side_effects=True, vmem_limit_bytes=60 * 1024 * 1024
+        ),
+    )(
+        prompt_rows,
+        query_weight,
+        cache_weight,
+        output_weight,
+        documents.reshape(1, -1),
+        page_table.reshape(1, -1),
+    )
+
+
+def fits(prompt_rows, query_weight, page_table):
+    tp_count = lax.axis_size("tp")
+    one_copy = tp_count == KV_HEADS
+    one_slot = prompt_rows.shape[0] // 4 == 1
+    return one_copy and one_slot and lax.axis_size("section") == 2
+
+
+def choose(prompt_rows, query_weight, cache_weight, output_weight, documents, page_table):
+    plan = fused_body if fits(prompt_rows, query_weight, page_table) else body
+    return plan(prompt_rows, query_weight, cache_weight, output_weight, documents, page_table)
+
+
 def solution(mesh):
     return jax.shard_map(
-        body,
+        choose,
         mesh=mesh,
         in_specs=(
             P(("parts", "section", "tp"), None),

time: 151 us -> 43.4 us (0.29)
  blocking collectives: 106 us -> 0 us
  Pallas kernels: 0 us -> 39.6 us
  matrix products: 21.1 us -> 0 us
  other arithmetic: 10.9 us -> 0 us
  starting transfers between devices: 5.83 us -> 0 us
  local copies, waits for them, and re-layouts: 4.85 us -> 2.87 us
    unnamed x1 -> x0, blocking collectives: 72.9 us -> none
    pallas_call x0 -> x1, Pallas kernels: none -> 39.6 us  [fused_body(): pl.pallas_call(functools.partial(fused_kernel, (tp_count, section_count,...]
    all_gather x1 -> x0, blocking collectives: 33.3 us -> none  [body(): piece = lax.all_gather(prompt_rows, 'tp', axis=0, tiled=True)]
    dot_general x4 -> x0, matrix products: 20.7 us -> none  [the longest x1 8.75 us: body(): jnp.dot(attention, output_weight, preferred_element_type=jnp.float32)]
    all_to_all x1 -> x0, starting transfers between devices: 5.82 us -> none  [body(): lax.all_to_all(outgoing, ('section', 'tp'), split_axis=0, concat_axis=2,...]
    gather x2 -> x0, other arithmetic: 4.6 us -> none  [body(): row_of = page_table[pages] * PAGE + offsets % PAGE]
    mul x2 -> x0, other arithmetic: 3.3 us -> none  [the longest x1 3.23 us: body(): row_of = page_table[pages] * PAGE + offsets % PAGE]
    gather x1 -> x0, local copies, waits for them, and re-layouts: 1.79 us -> none  [body(): row_of = page_table[pages] * PAGE + offsets % PAGE]
  transfers between devices with their start and end apart: 2 -> 0, of which waited for: 0 -> 0; matrix products, arithmetic and copies ran while one was open for 14% -> 0% of each run, Pallas kernels for 0% -> 0%
where the time goes in v1:
time: 43.4 us; the launch traced here: 43.1 us
  Pallas kernels  39.6 us (91%)
  local copies, waits for them, and re-layouts  2.87 us (7%)
  between operations  0.64 us (1%)
    pallas_call x1, Pallas kernels, fused_body(): pl.pallas_call(functools.partial(fused_kernel, (tp_count, section_count,...  39.6 us
    unnamed x2, local copies, waits for them, and re-layouts  2.87 us

profile of v1, /device:TPU:0, one launch (start us, length us, event | category | flops | bytes accessed | tf_op | source)
XLA Modules:
  0.0 43.1 jit_solution(10137028965461279705)
XLA Ops:
  0.6 39.6 %shard_map.77 = (bf16[4,8192]{1,0:T(4,128)(2,1)}, bf16[1,8,2048]{2,1,0:T(8,128)(2,1)}) custom-call(bf16[4,8192]{1,0:T(4,128)(2,1)} %rows_hbm.1, bf16[8192,1024]{1,0:T(8,128)(2,1)} %wq_hbm.1, bf16[1,8192,256]{2,1,0:T(8,128)(2,1)} %wkv_hbm.1, bf16[1024,8192]{1,0:T(8,128)(2,1)} %wo_hbm.1, s32[1,64]{1,0:T(1,128)} %bitcast.2, s32[1,12]{1,0:T(1,128)} %bitcast.3), custom_call_target="tpu_custom_call" | custom-call | tf_op jit(solution)/shard_map/pallas_call | solution.py:407
  40.2 1.5 %copy.10 = bf16[4,8192]{1,0:T(4,128)(2,1)} copy(bf16[4,8192]{1,0:T(4,128)(2,1)} %get-tuple-element.4) | data formatting | bytes 131072
  41.7 1.4 %copy.11 = bf16[1,8,2048]{2,1,0:T(8,128)(2,1)} copy(bf16[1,8,2048]{2,1,0:T(8,128)(2,1)} %get-tuple-element.5) | data formatting | bytes 65536

commit v2 on v1

--- a/solution.py
+++ b/solution.py
@@ -11,9 +11,12 @@
 KV_HEADS = 8
 HEAD = 128
 PAGE = 8
-K_CHUNKS = 4
-N_CHUNKS = 4
+K_CHUNKS = 2
+N_CHUNKS = 2
 MESH = pl.DeviceIdType.MESH
+FAR = (4, 6)
+NEAR = (1, 2, 3)
+HANDED = (5, 7)
 
 
 rope_base = 500000.0
@@ -140,6 +143,8 @@
     attn,
     sendbuf,
     recvbuf,
+    held,
+    joined,
     x_send,
     x_recv,
     x_local,
@@ -170,6 +175,13 @@
     def peer(distance):
         return lax.rem(me + distance, tp_count)
 
+    def mate(mask):
+        index = 0
+        for bit in (1, 2, 4):
+            digit = lax.rem(lax.div(me, bit), 2)
+            index = index + bit * (1 - digit if mask & bit else digit)
+        return index
+
     def device(sec, col):
         return (part, sec, col)
 
@@ -193,15 +205,30 @@
             wo_hbm.at[:, pl.ds(pl.multiple_of(n * nc, nc), nc)], wo.at[n], wo_sem.at[n]
         )
 
-    def row_copy(c, distance):
+    def row_copy(c, mask):
         return pltpu.make_async_remote_copy(
             src_ref=rows_hbm.at[:, pl.ds(pl.multiple_of(c * kc, kc), kc)],
             dst_ref=xbuf.at[c, me],
-            send_sem=x_send.at[c, distance],
-            recv_sem=x_recv.at[c, distance],
-            device_id=device(section, peer(distance)),
+            send_sem=x_send.at[c, mask],
+            recv_sem=x_recv.at[c, mask],
+            device_id=device(section, mate(mask)),
             device_id_type=MESH,
         )
+
+    def pass_on(c, mask):
+        return pltpu.make_async_remote_copy(
+            src_ref=xbuf.at[c, mate(mask)],
+            dst_ref=xbuf.at[c, mate(mask)],
+            send_sem=x_send.at[c, mask ^ 1],
+            recv_sem=x_recv.at[c, mask ^ 1],
+            device_id=device(section, mate(1)),
+            device_id_type=MESH,
+        )
+
+    def forward(c):
+        for mask in FAR:
+            row_copy(c, mask).wait_recv()
+            pass_on(c, mask).start()
 
     def own_rows(c):
         return pltpu.make_async_copy(
@@ -214,8 +241,8 @@
         own_rows(c).start()
     pl.semaphore_wait(barrier, owners - 1)
     for c in range(k_chunks):
-        for distance in range(1, tp_count):
-            row_copy(c, distance).start()
+        for mask in FAR + NEAR:
+            row_copy(c, mask).start()
     for c in range(1, k_chunks):
         for copy in weight_copies(c):
             copy.start()
@@ -268,10 +295,18 @@
     acc_q[...] = jnp.zeros_like(acc_q)
     acc_kv[...] = jnp.zeros_like(acc_kv)
 
+    forward(0)
+
     def project(c, carry):
+        @pl.when(c + 1 < k_chunks)
+        def _():
+            forward(c + 1)
+
         own_rows(c).wait()
-        for distance in range(1, tp_count):
-            row_copy(c, distance).wait_recv()
+        for mask in NEAR:
+            row_copy(c, mask).wait_recv()
+        for mask in FAR:
+            pass_on(c, mask).wait_recv()
         pieces = [xbuf[c, t].astype(jnp.float32) for t in range(tp_count)]
         block = jnp.concatenate(pieces, axis=0).astype(jnp.bfloat16)
         copies = weight_copies(c)
@@ -345,27 +380,41 @@
     for h in range(heads):
         attn[:, h * HEAD : (h + 1) * HEAD] = mixed[h * half_rows : (h + 1) * half_rows]
 
-    def sum_copy(n, distance):
-        to = peer(distance)
+    def sum_copy(n, mask):
         return pltpu.make_async_remote_copy(
-            src_ref=sendbuf.at[n, to],
-            dst_ref=recvbuf.at[n, me],
-            send_sem=r_send.at[n, distance],
-            recv_sem=r_recv.at[n, distance],
-            device_id=device(section, to),
+            src_ref=joined.at[n, FAR.index(mask)] if mask in FAR else sendbuf.at[n, mate(mask)],
+            dst_ref=recvbuf.at[n, mask],
+            send_sem=r_send.at[n, mask],
+            recv_sem=r_recv.at[n, mask],
+            device_id=device(section, mate(1 if mask in HANDED else mask)),
             device_id_type=MESH,
         )
+
+    def join(n):
+        for mask in FAR:
+            sum_copy(n, mask ^ 1).wait_recv()
+            term = held[n, mate(mask)] + recvbuf[n, mask ^ 1].astype(jnp.float32)
+            joined[n, FAR.index(mask)] = term.astype(jnp.bfloat16)
+            sum_copy(n, mask).start()
 
     def produce(n, carry):
         out_copy(n).wait()
         partial = jnp.dot(attn[...], wo[n], preferred_element_type=jnp.float32)
         for t in range(tp_count):
-            sendbuf[n, t] = partial[t * rows_dev : (t + 1) * rows_dev].astype(jnp.bfloat16)
-        for distance in range(1, tp_count):
-            sum_copy(n, distance).start()
+            piece = partial[t * rows_dev : (t + 1) * rows_dev]
+            held[n, t] = piece
+            sendbuf[n, t] = piece.astype(jnp.bfloat16)
+        for mask in HANDED + NEAR:
+            sum_copy(n, mask).start()
+
+        @pl.when(n >= 1)
+        def _():
+            join(n - 1)
+
         return carry
 
     lax.fori_loop(0, n_chunks, produce, 0)
+    join(n_chunks - 1)
 
     own_page.wait()
     for sec, distance in others:
@@ -374,19 +423,20 @@
         pool_ref[0, :, slot * HEAD : (slot + 1) * HEAD] = pagerecv[slot]
 
     for n in range(n_chunks):
-        total = sendbuf[n, me].astype(jnp.float32)
-        for distance in range(1, tp_count):
-            sum_copy(n, distance).wait_recv()
-            source = lax.rem(me + tp_count - distance, tp_count)
-            total += recvbuf[n, source].astype(jnp.float32)
+        total = held[n, me]
+        for mask in NEAR + FAR:
+            sum_copy(n, mask).wait_recv()
+            total += recvbuf[n, mask].astype(jnp.float32)
         out_ref[:, n * nc : (n + 1) * nc] = total.astype(jnp.bfloat16)
 
     for c in range(k_chunks):
-        for distance in range(1, tp_count):
-            row_copy(c, distance).wait_send()
+        for mask in FAR + NEAR:
+            row_copy(c, mask).wait_send()
+        for mask in FAR:
+            pass_on(c, mask).wait_send()
     for n in range(n_chunks):
-        for distance in range(1, tp_count):
-            sum_copy(n, distance).wait_send()
+        for mask in HANDED + NEAR + FAR:
+            sum_copy(n, mask).wait_send()
 
 
 def fused_body(prompt_rows, query_weight, cache_weight, output_weight, documents, page_table):
@@ -425,6 +475,8 @@
             pltpu.VMEM((half_rows, width), bf16),
             pltpu.VMEM((n_chunks, tp_count, rows_dev, nc), bf16),
             pltpu.VMEM((n_chunks, tp_count, rows_dev, nc), bf16),
+            pltpu.VMEM((n_chunks, tp_count, rows_dev, nc), f32),
+            pltpu.VMEM((n_chunks, 2, rows_dev, nc), bf16),
             dma((k_chunks, tp_count)),
             dma((k_chunks, tp_count)),
             dma((k_chunks,)),

time: 43.4 us -> 39.3 us (0.906)
  Pallas kernels: 39.6 us -> 35.6 us
    pallas_call x1, Pallas kernels: 39.6 us -> 35.6 us  [fused_body(): pl.pallas_call(functools.partial(fused_kernel, (tp_count, section_count,...]
where the time goes in v2:
time: 39.3 us; the launch traced here: 39.1 us
  Pallas kernels  35.6 us (91%)
  local copies, waits for them, and re-layouts  2.87 us (7%)
  between operations  0.64 us (2%)
    pallas_call x1, Pallas kernels, fused_body(): pl.pallas_call(functools.partial(fused_kernel, (tp_count, section_count,...  35.6 us
    unnamed x2, local copies, waits for them, and re-layouts  2.87 us

profile of v2, /device:TPU:0, one launch (start us, length us, event | category | flops | bytes accessed | tf_op | source)
XLA Modules:
  0.0 39.1 jit_solution(13374958690868578304)
XLA Ops:
  0.6 35.6 %shard_map.77 = (bf16[4,8192]{1,0:T(4,128)(2,1)}, bf16[1,8,2048]{2,1,0:T(8,128)(2,1)}) custom-call(bf16[4,8192]{1,0:T(4,128)(2,1)} %rows_hbm.1, bf16[8192,1024]{1,0:T(8,128)(2,1)} %wq_hbm.1, bf16[1,8192,256]{2,1,0:T(8,128)(2,1)} %wkv_hbm.1, bf16[1024,8192]{1,0:T(8,128)(2,1)} %wo_hbm.1, s32[1,64]{1,0:T(1,128)} %bitcast.2, s32[1,12]{1,0:T(1,128)} %bitcast.3), custom_call_target="tpu_custom_call" | custom-call | tf_op jit(solution)/shard_map/pallas_call | solution.py:457
  36.2 1.5 %copy.10 = bf16[4,8192]{1,0:T(4,128)(2,1)} copy(bf16[4,8192]{1,0:T(4,128)(2,1)} %get-tuple-element.4) | data formatting | bytes 131072
  37.7 1.4 %copy.11 = bf16[1,8,2048]{2,1,0:T(8,128)(2,1)} copy(bf16[1,8,2048]{2,1,0:T(8,128)(2,1)} %get-tuple-element.5) | data formatting | bytes 65536

commit v3 on v2

--- a/solution.py
+++ b/solution.py
@@ -295,6 +295,15 @@
     acc_q[...] = jnp.zeros_like(acc_q)
     acc_kv[...] = jnp.zeros_like(acc_kv)
 
+    kv_copy = pltpu.make_async_remote_copy(
+        src_ref=kv_all.at[section],
+        dst_ref=kv_all.at[section],
+        send_sem=kv_send,
+        recv_sem=kv_recv,
+        device_id=device(1 - section, me),
+        device_id_type=MESH,
+    )
+
     forward(0)
 
     def project(c, carry):
@@ -312,23 +321,20 @@
         copies = weight_copies(c)
         copies[0].wait()
         acc_kv[...] += jnp.dot(block, wkv[c], preferred_element_type=jnp.float32)
+
+        @pl.when(c == k_chunks - 1)
+        def _():
+            keys_own = rotate_rows(acc_kv[:, :HEAD])
+            kv_own = jnp.concatenate([keys_own, acc_kv[:, HEAD:]], axis=1)
+            kv_all[section] = kv_own.astype(jnp.bfloat16)
+            kv_copy.start()
+
         copies[1].wait()
         acc_q[...] += jnp.dot(block, wq[c], preferred_element_type=jnp.float32)
         return carry
 
     lax.fori_loop(0, k_chunks, project, 0)
 
-    keys_own = rotate_rows(acc_kv[:, :HEAD])
-    kv_all[section] = jnp.concatenate([keys_own, acc_kv[:, HEAD:]], axis=1).astype(jnp.bfloat16)
-    kv_copy = pltpu.make_async_remote_copy(
-        src_ref=kv_all.at[section],
-        dst_ref=kv_all.at[section],
-        send_sem=kv_send,
-        recv_sem=kv_recv,
-        device_id=device(1 - section, me),
-        device_id_type=MESH,
-    )
-    kv_copy.start()
     queries = jnp.concatenate(
         [rotate_rows(acc_q[:, h * HEAD : (h + 1) * HEAD]) for h in range(heads)], axis=0
     ).astype(jnp.bfloat16)
@@ -454,7 +460,7 @@
     dma = pltpu.SemaphoreType.DMA
     anywhere = pl.BlockSpec(memory_space=pl.ANY)
     local = pl.BlockSpec(memory_space=pltpu.VMEM)
-    return pl.pallas_call(
+    summed, pages = pl.pallas_call(
         functools.partial(fused_kernel, (tp_count, section_count, k_chunks, n_chunks)),
         out_shape=(
             jax.ShapeDtypeStruct((rows_dev, out_width), bf16),
@@ -501,6 +507,27 @@
         documents.reshape(1, -1),
         page_table.reshape(1, -1),
     )
+    return pl.pallas_call(
+        write_kernel,
+        out_shape=(
+            jax.ShapeDtypeStruct(summed.shape, bf16),
+            jax.ShapeDtypeStruct(pages.shape, bf16),
+        ),
+        in_specs=[local] * 2,
+        out_specs=(anywhere, anywhere),
+        scratch_shapes=[dma((2,))],
+    )(summed, pages)
+
+
+def write_kernel(summed_ref, pages_ref, out_ref, pool_ref, sems):
+    copies = (
+        pltpu.make_async_copy(summed_ref, out_ref, sems.at[0]),
+        pltpu.make_async_copy(pages_ref, pool_ref, sems.at[1]),
+    )
+    for copy in copies:
+        copy.start()
+    for copy in copies:
+        copy.wait()
 
 
 def fits(prompt_rows, query_weight, page_table):

time: 39.3 us -> 36.5 us (0.929)
  local copies, waits for them, and re-layouts: 2.87 us -> 0 us
    unnamed x2 -> x0, local copies, waits for them, and re-layouts: 2.87 us -> none
    pallas_call x0 -> x1, Pallas kernels: none -> 1.49 us  [fused_body(): pl.pallas_call(write_kernel, out_shape=(jax.ShapeDtypeStruct(summed.shape...]
    pallas_call x1, Pallas kernels: 35.6 us -> 34.2 us  [fused_body(): pl.pallas_call(functools.partial(fused_kernel, (tp_count, section_count,...]
where the time goes in v3:
time: 36.5 us; the launch traced here: 36.4 us
  Pallas kernels  35.7 us (98%)
  between operations  0.64 us (2%)
    pallas_call x1, Pallas kernels, fused_body(): pl.pallas_call(functools.partial(fused_kernel, (tp_count, section_count,...  34.2 us
    pallas_call x1, Pallas kernels, fused_body(): pl.pallas_call(write_kernel, out_shape=(jax.ShapeDtypeStruct(summed.shape...  1.49 us

profile of v3, /device:TPU:0, one launch (start us, length us, event | category | flops | bytes accessed | tf_op | source)
XLA Modules:
  0.0 36.4 jit_solution(14362296126964264496)
XLA Ops:
  0.6 34.2 %shard_map.77 = (bf16[4,8192]{1,0:T(4,128)(2,1)}, bf16[1,8,2048]{2,1,0:T(8,128)(2,1)}) custom-call(bf16[4,8192]{1,0:T(4,128)(2,1)} %rows_hbm.1, bf16[8192,1024]{1,0:T(8,128)(2,1)} %wq_hbm.1, bf16[1,8192,256]{2,1,0:T(8,128)(2,1)} %wkv_hbm.1, bf16[1024,8192]{1,0:T(8,128)(2,1)} %wo_hbm.1, s32[1,64]{1,0:T(1,128)} %bitcast.2, s32[1,12]{1,0:T(1,128)} %bitcast.3), custom_call_target="tpu_custom_call" | custom-call | tf_op jit(solution)/shard_map/pallas_call | solution.py:463
  34.9 1.5 %shard_map.78 = (bf16[4,8192]{1,0:T(4,128)(2,1)}, bf16[1,8,2048]{2,1,0:T(8,128)(2,1)}) custom-call(bf16[4,8192]{1,0:T(4,128)(2,1)} %get-tuple-element.4.summed_ref, bf16[1,8,2048]{2,1,0:T(8,128)(2,1)} %get-tuple-element.5.pages_ref), custom_call_target="tpu_custom_call" | custom-call | tf_op jit(solution)/shard_map/pallas_call | solution.py:510
